TPU v7x, 128 devices: a whole 4x4x4 slice. The times are simulated.
128 devices in a mesh: replica: 8 (over z_hi, y), tensor: 16 (over x, z_lo, core).
Axes of the slice: x: 4, y: 4, z: 4 (z_hi: 2, z_lo: 2; z = z_hi * 2 + z_lo), core: 2. Of those that a mesh axis runs over, the one named last changes fastest.
Arguments:
- queries: bfloat16 [1024, 8192], P('replica', 'tensor'), may hold values from -200 to 200
- new_kv: bfloat16 [1024, 1024], P('replica'), may hold values from -8 to 8
- kv_pool: bfloat16 [1024, 64, 1024], P(('replica', 'tensor')), may hold values from -6 to 6
- anchor: int32 [8, 8], replicated, may hold values from 0 to 7, as said below
- page_table: int32 [64, 16], replicated, may hold values from 0 to 7, as said below
- prefix_len: int32 [64], replicated, may hold values from 1 to 1024, 32768 in all
- turn_rows: int32 [8, 8], replicated, may hold values from 1 to 32, 128 in all within a row
- out_weight: bfloat16 [8192, 16384], P('tensor', 'replica'), may hold values from -0.5 to 0.5
- residual: bfloat16 [1024, 16384], P(None, 'replica'), may hold values from -400 to 400
- norm_gain: bfloat16 [16384], P('replica'), may hold values from 0.099609375 to 1.8984375
- gate_up: bfloat16 [16384, 2, 26624], P('replica', None, 'tensor'), may hold values from -0.046875 to 0.046875
Outputs:
- hidden: bfloat16 [1024, 26624], P('replica', 'tensor')
Inputs may be any that keep to these rules, and one draw needn't show every extreme that they name: Slot j of new replica d holds session anchor[d, j] of old replica j; for each old replica, the 8 slots that come from it name each of its 8 sessions exactly once. `page_table`: row o * 8 + s lists the pages of session s of old replica o: entry k is a local page index on device k of that replica's 16 tensor devices, whose pages are numbered (o * 16 + k) * 8 + index in kv_pool; on each device the 8 sessions use distinct pages. `prefix_len`: indexed by d * 8 + j for slot j of new replica d. `turn_rows`: each replica's entries sum to 128.
All inputs are finite; a program needn't handle non-finite values.
Results may differ from a plain program's by a relative error of at most 0.0064.
Values may be sent and summed in bfloat16 or wider, within the bound.
A program may use at most 128 MiB of HBM per device.

v0:
```python
import jax
import jax.numpy as jnp
import numpy as np
from jax import lax
from jax.sharding import PartitionSpec as P

D = 16384
HD = 128
HEADS = 64
KVH = 4
PAGE = 64
SHARE = 1
ROWS = 128
GROUP = 16
EPSILON = 1e-05


def per_device(
    queries,
    new_kv,
    kv_pool,
    anchor,
    page_table,
    prefix_len,
    turn_rows,
    out_weight,
    residual,
    norm_gain,
    gate_up,
):
    replicas = lax.axis_size("replica")
    tensors = lax.axis_size("tensor")
    replica_idx = lax.axis_index("replica")
    tensor_idx = lax.axis_index("tensor")
    sessions = SHARE * replicas
    heads_local = HEADS // tensors
    pair_width = 2 * HD
    cached_len = tensors * PAGE
    owner_head = np.arange(tensors) * heads_local // GROUP
    from_here = lax.dynamic_slice_in_dim(anchor, replica_idx * SHARE, SHARE, 1)
    table_rows = lax.dynamic_slice_in_dim(page_table, replica_idx * sessions, sessions, 0)
    my_column = lax.dynamic_slice_in_dim(table_rows, tensor_idx, 1, 1)[:, 0]
    page_index = jnp.take(my_column, from_here.reshape(-1), axis=0)
    chosen = jnp.take(kv_pool, page_index, axis=0).reshape(replicas, SHARE, PAGE, KVH, pair_width)
    half = PAGE // 2
    lanes_per_head = tensors // KVH
    outgoing = jnp.transpose(chosen.reshape(replicas, 2, half, KVH, pair_width), (0, 3, 1, 2, 4))
    outgoing = jnp.broadcast_to(
        outgoing[:, :, None], (replicas, KVH, lanes_per_head // 2, 2, half, pair_width)
    ).reshape(replicas * tensors, SHARE, half, pair_width)
    arrived = lax.all_to_all(
        outgoing, ("replica", "tensor"), split_axis=0, concat_axis=0, tiled=True
    )
    partner = lax.ppermute(arrived, "tensor", [(i, i ^ 1) for i in range(tensors)])
    arrived = jnp.concatenate([arrived, partner], axis=2)
    arrived = arrived.reshape(replicas, tensors, SHARE, PAGE, pair_width)
    prefix_blocks = jnp.transpose(arrived, (0, 2, 1, 3, 4)).reshape(
        sessions, cached_len, pair_width
    )
    kv_group = tensor_idx * heads_local // GROUP
    fresh_pair = lax.dynamic_slice_in_dim(new_kv, kv_group * pair_width, pair_width, 1)
    rows_here = queries.shape[0]
    slot_rows = ROWS // 4
    query_heads = queries.reshape(rows_here, heads_local, HD)
    counts = lax.dynamic_slice_in_dim(turn_rows, replica_idx, 1, 0)[0]
    bounds = jnp.cumsum(counts, dtype=jnp.int32)
    starts = bounds - counts
    row_ids = jnp.arange(rows_here, dtype=jnp.int32)
    row_slot = jnp.sum(
        (row_ids[:, None] >= bounds[None, :]).astype(jnp.int32), axis=1, dtype=jnp.int32
    )
    offsets = jnp.arange(slot_rows, dtype=jnp.int32)
    padded_index = jnp.minimum(starts[:, None] + offsets[None, :], rows_here - 1).reshape(-1)
    slot_queries = jnp.take(query_heads, padded_index, axis=0).reshape(
        sessions, slot_rows, heads_local, HD
    )
    slot_fresh = jnp.take(fresh_pair, padded_index, axis=0).reshape(sessions, slot_rows, pair_width)
    lengths = lax.dynamic_slice_in_dim(prefix_len, replica_idx * sessions, sessions, 0)
    key_ids = jnp.arange(cached_len, dtype=jnp.int32)
    key_pos = key_ids // PAGE * PAGE + (key_ids % PAGE + tensor_idx % 2 * half) % PAGE
    prefix_mask = (key_pos[None, :] < lengths[:, None])[:, None, :]
    fresh_mask = (offsets[None, None, :] <= offsets[None, :, None]) & (
        offsets[None, None, :] < counts[:, None, None]
    )
    score_scale = HD ** (-0.5)
    prefix_scores = (
        jnp.einsum(
            "smhd,skd->hsmk",
            slot_queries,
            prefix_blocks[:, :, :HD],
            preferred_element_type=jnp.float32,
        )
        * score_scale
    )
    fresh_scores = (
        jnp.einsum(
            "smhd,snd->hsmn",
            slot_queries,
            slot_fresh[:, :, :HD],
            preferred_element_type=jnp.float32,
        )
        * score_scale
    )
    prefix_scores = jnp.where(prefix_mask[None], prefix_scores, -jnp.inf)
    fresh_scores = jnp.where(fresh_mask[None], fresh_scores, -jnp.inf)
    row_peak = jnp.maximum(jnp.max(prefix_scores, axis=3), jnp.max(fresh_scores, axis=3))
    prefix_weights = jnp.exp(prefix_scores - row_peak[..., None])
    fresh_weights = jnp.exp(fresh_scores - row_peak[..., None])
    denominator = jnp.sum(prefix_weights, axis=3) + jnp.sum(fresh_weights, axis=3)
    mixed_values = jnp.einsum(
        "hsmk,skd->smhd",
        prefix_weights.astype(jnp.bfloat16),
        prefix_blocks[:, :, HD:],
        preferred_element_type=jnp.float32,
    )
    mixed_values = mixed_values + jnp.einsum(
        "hsmn,snd->smhd",
        fresh_weights.astype(jnp.bfloat16),
        slot_fresh[:, :, HD:],
        preferred_element_type=jnp.float32,
    )
    slot_attended = (mixed_values / jnp.transpose(denominator, (1, 2, 0))[..., None]).astype(
        jnp.bfloat16
    )
    slot_attended = slot_attended.reshape(sessions * slot_rows, heads_local * HD)
    back_index = row_slot * slot_rows + row_ids - jnp.take(starts, row_slot, axis=0)
    attended = jnp.take(slot_attended, back_index, axis=0)
    gathered = lax.all_to_all(
        jnp.broadcast_to(attended[None], (replicas,) + attended.shape),
        "replica",
        split_axis=0,
        concat_axis=0,
        tiled=True,
    ).reshape(replicas * rows_here, attended.shape[1])
    partial_out = jnp.dot(gathered, out_weight, preferred_element_type=jnp.float32)
    all_rows = partial_out.shape[0]
    width = partial_out.shape[1]
    part_rows = all_rows // tensors
    head_parts = lax.all_to_all(
        partial_out.astype(jnp.bfloat16).reshape(tensors, part_rows, width),
        "tensor",
        split_axis=0,
        concat_axis=0,
        tiled=True,
    )
    head_sum = jnp.sum(head_parts.astype(jnp.float32), axis=0)
    my_residual = lax.dynamic_slice_in_dim(residual, tensor_idx * part_rows, part_rows, 0)
    carried = my_residual.astype(jnp.float32) + head_sum
    gain_row = norm_gain.astype(jnp.float32)
    own_squares = jnp.sum(carried * carried, axis=1)
    squares = jnp.sum(
        lax.all_to_all(
            jnp.broadcast_to(own_squares[None], (replicas,) + own_squares.shape),
            "replica",
            split_axis=0,
            concat_axis=0,
            tiled=True,
        ),
        axis=0,
    )
    normed_part = (carried * lax.rsqrt(squares / D + EPSILON)[:, None] * gain_row[None, :]).astype(
        jnp.bfloat16
    )
    normed = lax.all_gather(normed_part, "tensor", axis=0, tiled=True)
    weights_local = gate_up.reshape(gate_up.shape[0], 2 * gate_up.shape[2])
    slab = jnp.dot(normed, weights_local, preferred_element_type=jnp.float32)
    slab_parts = lax.all_to_all(
        slab.astype(jnp.bfloat16).reshape(replicas, rows_here, slab.shape[1]),
        "replica",
        split_axis=0,
        concat_axis=0,
        tiled=True,
    )
    summed = jnp.sum(slab_parts.astype(jnp.float32), axis=0)
    ff_here = gate_up.shape[2]
    gate = summed[:, :ff_here]
    up = summed[:, ff_here:]
    return (jax.nn.silu(gate) * up).astype(jnp.bfloat16)


def solution(mesh):
    placed = (
        P("replica", "tensor"),
        P("replica", None),
        P(("replica", "tensor"), None, None),
        P(),
        P(),
        P(),
        P(),
        P("tensor", "replica"),
        P(None, "replica"),
        P("replica"),
        P("replica", None, "tensor"),
    )
    return jax.shard_map(
        per_device, mesh=mesh, in_specs=placed, out_specs=P("replica", "tensor"), check_vma=False
    )
```

profile of v0, /device:TPU:1, one launch (start us, length us, event | category | flops | bytes accessed | tf_op | source)
XLA Modules:
  0.0 329.1 jit_solution(6830536024076237477)
XLA Ops:
  6.5 0.9 constant_dynamic-slice_fusion.1
  7.6 0.8 dynamic-slice_bitcast_fusion
  9.0 2.8 gather_fusion.1
  11.8 1.9 gather.38
  14.4 1.6 broadcast_in_dim.111
  16.0 11.9 %all-to-all-start = ((bf16[128,1,32,256]{3,2,1,0:T(8,128)(2,1)}), bf16[128,1,32,256]{3,2,1,0:T(8,128)(2,1)}, u32[]{:S(2)}, u32[]{:S(2)}) async-start(bf16[128,1,32,256]{3,2,1,0:T(8,128)(2,1)} %bitcast.141), calls=%async_computation | async-start | bytes 4194304 | tf_op jit(solution)/shard_map/all_to_all | solution.py:51
  30.4 0.8 constant_dynamic-slice_fusion
  31.2 26.0 %all-to-all-done = bf16[128,1,32,256]{3,2,1,0:T(8,128)(2,1)} async-done(((bf16[128,1,32,256]{3,2,1,0:T(8,128)(2,1)}), bf16[128,1,32,256]{3,2,1,0:T(8,128)(2,1)}, u32[]{:S(2)}, u32[]{:S(2)}) %all-to-all-start) | async-done | bytes 2097184 | tf_op jit(solution)/shard_map/all_to_all | solution.py:51
  57.2 1.3 collective-permute-start
  58.7 1.2 gather_fusion.3
  59.9 1.0 gather_fusion.2
  61.0 5.0 %compare_and_fusion.1 = (pred[128]{0:T(512)(128)(4,1)S(1)}, s32[128]{0:T(128)S(1)}) fusion(s32[128]{0:T(128)S(1)} %convert_reduce_fusion.2, s32[]{:T(128)} %bitcast.12, s32[]{:T(128)} %bitcast.11, s32[]{:T(128)} %bitcast.10, s32[]{:T(128)} %bitcast.9, s32[]{:T(128)} %bitcast.8, s32[]{:T(128)} %bitcast.7, s32[]{:T(128)} %bitcast.6, s32[]{:T(128)} %bitcast.5), kind=kLoop, calls=%fused_computation.99 | loop fusion | flops 4224 | bytes 1184 | tf_op jit(solution)/shard_map/jit(_take)/and | solution.py:127
  67.1 2.7 pad_maximum_fusion
  69.8 0.9 bitcast_reduce_fusion
  71.1 1.1 fusion.1
  72.2 1.4 fusion.21
  73.8 0.8 gather_fusion.4
  74.9 20.1 %all_to_all.26 = bf16[8,128,512]{2,1,0:T(8,128)(2,1)S(1)} all-to-all(bf16[8,128,512]{2,1,0:T(8,128)(2,1)S(1)} %broadcast_in_dim.122), channel_id=1, replica_groups=mesh['replica'=8,'tensor'=16] {'replica'}, dimensions={0} | all-to-all | bytes 2097152 | tf_op jit(solution)/shard_map/all_to_all | solution.py:128
  95.0 4.3 %convolution_convert_fusion.1 = bf16[1024,2048]{1,0:T(8,128)(2,1)} fusion(bf16[1024,512]{1,0:T(8,128)(2,1)S(1)} %bitcast.147, bf16[512,2048]{1,0:T(8,128)(2,1)S(1)} %copy-done), kind=kOutput, calls=%fused_computation.13 | convolution fusion | flops 2149580800 | bytes 7340032 | tf_op jit(solution)/shard_map/dot_general | solution.py:135
  99.3 5.1 %all-to-all-start.2 = ((bf16[16,64,2048]{2,1,0:T(8,128)(2,1)}), bf16[16,64,2048]{2,1,0:T(8,128)(2,1)}, u32[]{:S(2)}, u32[]{:S(2)}) async-start(bf16[16,64,2048]{2,1,0:T(8,128)(2,1)} %bitcast.146), calls=%async_computation.2 | async-start | bytes 8388608 | tf_op jit(solution)/shard_map/all_to_all | solution.py:139
  104.3 52.6 %all-to-all-done.2 = bf16[16,64,2048]{2,1,0:T(8,128)(2,1)} async-done(((bf16[16,64,2048]{2,1,0:T(8,128)(2,1)}), bf16[16,64,2048]{2,1,0:T(8,128)(2,1)}, u32[]{:S(2)}, u32[]{:S(2)}) %all-to-all-start.2) | async-done | bytes 4194336 | tf_op jit(solution)/shard_map/all_to_all | solution.py:139
  157.0 3.0 convert_reduce_fusion.1
  160.0 1.1 multiply_reduce_fusion
  161.7 3.3 %all-to-all-start.3 = ((f32[8,1,64]{2,1,0:T(1,128)}), f32[8,1,64]{2,1,0:T(1,128)S(1)}, u32[]{:S(2)}, u32[]{:S(2)}) async-start(f32[8,1,64]{2,1,0:T(1,128)} %broadcast_in_dim.123), calls=%async_computation.3 | async-start | bytes 8192 | tf_op jit(solution)/shard_map/all_to_all | solution.py:152
  165.3 6.1 %all-to-all-done.3 = f32[8,1,64]{2,1,0:T(1,128)S(1)} async-done(((f32[8,1,64]{2,1,0:T(1,128)}), f32[8,1,64]{2,1,0:T(1,128)S(1)}, u32[]{:S(2)}, u32[]{:S(2)}) %all-to-all-start.3) | async-done | bytes 2080 | tf_op jit(solution)/shard_map/all_to_all | solution.py:152
  171.5 1.8 multiply_convert_fusion
  173.2 14.2 %copy.57 = bf16[256,8,2,1664]{3,1,2,0:T(8,128)(2,1)} copy(bf16[256,8,2,1664]{3,2,1,0:T(2,128)(2,1)} %bitcast.139) | data formatting | bytes 27262976
  187.5 27.6 %all-gather.2.cloned.1.call-done = bf16[1024,2048]{1,0:T(8,128)(2,1)} async-done(((bf16[64,2048]{1,0:T(8,128)(2,1)}), bf16[1024,2048]{1,0:T(8,128)(2,1)}) %all-gather.2.cloned.1.call-update) | async-done | bytes 4194320 | tf_op jit(solution)/shard_map/all_gather | solution.py:164
  215.1 19.7 %convolution_convert_fusion = bf16[1024,3328]{1,0:T(8,128)(2,1)S(1)} fusion(bf16[1024,2048]{1,0:T(8,128)(2,1)} %all-gather.2.cloned.1.call-done, bf16[2048,3328]{1,0:T(8,128)(2,1)} %bitcast.140), kind=kOutput, calls=%fused_computation.7 | convolution fusion | flops 13962051584 | bytes 24641536 | tf_op jit(solution)/shard_map/dot_general | solution.py:166
  234.8 85.5 %all_to_all.27 = bf16[8,128,3328]{2,1,0:T(8,128)(2,1)S(1)} all-to-all(bf16[8,128,3328]{2,1,0:T(8,128)(2,1)S(1)} %bitcast.142), channel_id=1, replica_groups=mesh['replica'=8,'tensor'=16] {'replica'}, dimensions={0} | all-to-all | bytes 13631488 | tf_op jit(solution)/shard_map/all_to_all | solution.py:167
  320.3 1.0 convert_reduce_fusion
  321.3 1.0 fusion.24
  (55 shorter events, 6.9 us)
Async XLA Ops:
  6.5 88.4 %copy-start = (bf16[512,2048]{1,0:T(8,128)(2,1)S(1)}, bf16[512,2048]{1,0:T(8,128)(2,1)}, u32[]{:S(2)}) copy-start(bf16[512,2048]{1,0:T(8,128)(2,1)} %param.18) | copy-start | bytes 6291460
  14.4 44.2 %copy-start.4 = (s32[64]{0:T(128)S(1)}, s32[64]{0:T(128)}, u32[]{:S(2)}) copy-start(s32[64]{0:T(128)} %param.16) | copy-start | bytes 772
  14.4 44.3 %copy-start.2 = (bf16[128,512]{1,0:T(8,128)(2,1)S(1)}, bf16[128,512]{1,0:T(8,128)(2,1)}, u32[]{:S(2)}) copy-start(bf16[128,512]{1,0:T(8,128)(2,1)} %param.11) | copy-start | bytes 393220
  16.0 41.3 %all-to-all-start = ((bf16[128,1,32,256]{3,2,1,0:T(8,128)(2,1)}), bf16[128,1,32,256]{3,2,1,0:T(8,128)(2,1)}, u32[]{:S(2)}, u32[]{:S(2)}) async-start(bf16[128,1,32,256]{3,2,1,0:T(8,128)(2,1)} %bitcast.141), calls=%async_computation | async-start | bytes 4194304 | tf_op jit(solution)/shard_map/all_to_all | solution.py:51
  57.2 9.8 %collective-permute-start = (bf16[128,1,32,256]{3,2,1,0:T(8,128)(2,1)}, bf16[128,1,32,256]{3,2,1,0:T(8,128)(2,1)}, u32[]{:S(2)}, u32[]{:S(2)}) collective-permute-start(bf16[128,1,32,256]{3,2,1,0:T(8,128)(2,1)} %all-to-all-done), channel_id=1, source_target_pairs={{0,1},{1,0},{2,3},{3,2},{4,5},{5,4},{6,7},{7,6},{8,9},{9,8},{10,11... | collective-permute-start | bytes 6291464 | tf_op jit(solution)/shard_map/ppermute | solution.py:54
  99.3 57.7 %all-to-all-start.2 = ((bf16[16,64,2048]{2,1,0:T(8,128)(2,1)}), bf16[16,64,2048]{2,1,0:T(8,128)(2,1)}, u32[]{:S(2)}, u32[]{:S(2)}) async-start(bf16[16,64,2048]{2,1,0:T(8,128)(2,1)} %bitcast.146), calls=%async_computation.2 | async-start | bytes 8388608 | tf_op jit(solution)/shard_map/all_to_all | solution.py:139
  104.3 60.9 %copy-start.3 = (bf16[2048]{0:T(1024)(128)(2,1)S(1)}, bf16[2048]{0:T(1024)(128)(2,1)}, u32[]{:S(2)}) copy-start(bf16[2048]{0:T(1024)(128)(2,1)} %param.20) | copy-start | bytes 12292
  161.7 9.7 %all-to-all-start.3 = ((f32[8,1,64]{2,1,0:T(1,128)}), f32[8,1,64]{2,1,0:T(1,128)S(1)}, u32[]{:S(2)}, u32[]{:S(2)}) async-start(f32[8,1,64]{2,1,0:T(1,128)} %broadcast_in_dim.123), calls=%async_computation.3 | async-start | bytes 8192 | tf_op jit(solution)/shard_map/all_to_all | solution.py:152
  165.0 50.0 %all-gather.2.cloned.1.call-start = ((), (), s32[]{:S(2)}) async-start(), calls=%async_computation.5 | async-start | bytes 4456448 | tf_op jit(solution)/shard_map/all_gather | solution.py:164
  234.8 87.5 %copy-start.1 = (bf16[512,2048]{1,0:T(8,128)(2,1)S(1)}, bf16[512,2048]{1,0:T(8,128)(2,1)}, u32[]{:S(2)}) copy-start(bf16[512,2048]{1,0:T(8,128)(2,1)} %param.18) | copy-start | bytes 6291460
Sparse Core Ops, SparseCore 0:
  173.4 41.6 all-gather.1
where the time goes:
time: 330 us; the launch traced here: 329 us
  waiting for transfers between devices  112 us (34%)
  blocking collectives  106 us (32%)
  local copies, waits for them, and re-layouts  29.4 us (9%)
  matrix products  27.2 us (8%)
  starting transfers between devices  21.9 us (7%)
  other arithmetic  19 us (6%)
  between operations  13.7 us (4%)
    all_to_all x1, blocking collectives, per_device(): lax.all_to_all(slab.astype(jnp.bfloat16).reshape(replicas, rows_here, sla...  85.5 us
    all_to_all x1, waiting for transfers between devices, per_device(): lax.all_to_all(partial_out.astype(jnp.bfloat16).reshape(tensors, part_row...  52.6 us
    all_gather x1, waiting for transfers between devices, per_device(): normed = lax.all_gather(normed_part, 'tensor', axis=0, tiled=True)  27.6 us
    all_to_all x1, waiting for transfers between devices, per_device(): lax.all_to_all(outgoing, ('replica', 'tensor'), split_axis=0, concat_axis...  26 us
    all_to_all x1, blocking collectives, per_device(): lax.all_to_all(jnp.broadcast_to(attended[None], (replicas,) + attended.sh...  20.1 us
    dot_general x1, matrix products, per_device(): slab = jnp.dot(normed, weights_local, preferred_element_type=jnp.float32)  19.7 us
    unnamed x13, local copies, waits for them, and re-layouts  14.4 us
    all_to_all x1, starting transfers between devices, per_device(): lax.all_to_all(outgoing, ('replica', 'tensor'), split_axis=0, concat_axis...  11.9 us
  transfers between devices with their start and end apart: 5, of which 4 were waited for; matrix products, arithmetic and copies ran while one was open for 8% of the time, Pallas kernels for 0%

commit v1 on v0

--- a/solution.py
+++ b/solution.py
@@ -161,7 +161,10 @@
     normed_part = (carried * lax.rsqrt(squares / D + EPSILON)[:, None] * gain_row[None, :]).astype(
         jnp.bfloat16
     )
-    normed = lax.all_gather(normed_part, "tensor", axis=0, tiled=True)
+    normed = jnp.concatenate(
+        jax.lax.all_to_all(jnp.stack([normed_part] * jax.lax.axis_size("tensor")), "tensor", 0, 0),
+        axis=0,
+    )
     weights_local = gate_up.reshape(gate_up.shape[0], 2 * gate_up.shape[2])
     slab = jnp.dot(normed, weights_local, preferred_element_type=jnp.float32)
     slab_parts = lax.all_to_all(

time: 330 us -> 344 us (1.042)
  the two profiles are of different devices: /device:TPU:1 before, /device:TPU:36 now
where the time goes in v1:
time: 344 us; the launch traced here: 343 us
  waiting for transfers between devices  134 us (39%)
  blocking collectives  103 us (30%)
  local copies, waits for them, and re-layouts  31.9 us (9%)
  starting transfers between devices  27.6 us (8%)
  matrix products  27.2 us (8%)
  other arithmetic  18.2 us (5%)
    all_to_all x1, blocking collectives, per_device(): lax.all_to_all(slab.astype(jnp.bfloat16).reshape(replicas, rows_here, sla...  82.5 us
    all_to_all x1, waiting for transfers between devices, per_device(): lax.all_to_all(partial_out.astype(jnp.bfloat16).reshape(tensors, part_row...  57.9 us
    all_to_all x1, waiting for transfers between devices, per_device(): jax.lax.all_to_all(jnp.stack([normed_part] * jax.lax.axis_size('tensor'))...  44.9 us
    all_to_all x1, waiting for transfers between devices, per_device(): lax.all_to_all(outgoing, ('replica', 'tensor'), split_axis=0, concat_axis...  23.9 us
    all_to_all x1, blocking collectives, per_device(): lax.all_to_all(jnp.broadcast_to(attended[None], (replicas,) + attended.sh...  20.8 us
    dot_general x1, matrix products, per_device(): slab = jnp.dot(normed, weights_local, preferred_element_type=jnp.float32)  19.7 us
    unnamed x13, local copies, waits for them, and re-layouts  14.4 us
    all_to_all x1, starting transfers between devices, per_device(): lax.all_to_all(outgoing, ('replica', 'tensor'), split_axis=0, concat_axis...  10.7 us
  transfers between devices with their start and end apart: 5, of which 4 were waited for; matrix products, arithmetic and copies ran while one was open for 8% of the time, Pallas kernels for 0%

profile of v1, /device:TPU:36, one launch (start us, length us, event | category | flops | bytes accessed | tf_op | source)
XLA Modules:
  0.0 342.6 jit_solution(5088800375408503374)
XLA Ops:
  0.0 0.9 constant_dynamic-slice_fusion.1
  2.5 2.8 gather_fusion.1
  5.3 1.9 gather.38
  7.9 1.6 broadcast_in_dim.111
  9.5 10.7 %all-to-all-start = ((bf16[128,1,32,256]{3,2,1,0:T(8,128)(2,1)}), bf16[128,1,32,256]{3,2,1,0:T(8,128)(2,1)}, u32[]{:S(2)}, u32[]{:S(2)}) async-start(bf16[128,1,32,256]{3,2,1,0:T(8,128)(2,1)} %bitcast.142), calls=%async_computation | async-start | bytes 4194304 | tf_op jit(solution)/shard_map/all_to_all | solution.py:51
  22.6 0.8 constant_dynamic-slice_fusion
  23.4 23.9 %all-to-all-done = bf16[128,1,32,256]{3,2,1,0:T(8,128)(2,1)} async-done(((bf16[128,1,32,256]{3,2,1,0:T(8,128)(2,1)}), bf16[128,1,32,256]{3,2,1,0:T(8,128)(2,1)}, u32[]{:S(2)}, u32[]{:S(2)}) %all-to-all-start) | async-done | bytes 2097184 | tf_op jit(solution)/shard_map/all_to_all | solution.py:51
  47.9 1.2 gather_fusion.3
  49.1 1.0 gather_fusion.2
  50.2 5.0 %compare_and_fusion.1 = (pred[128]{0:T(512)(128)(4,1)S(1)}, s32[128]{0:T(128)S(1)}) fusion(s32[128]{0:T(128)S(1)} %convert_reduce_fusion.2, s32[]{:T(128)} %bitcast.12, s32[]{:T(128)} %bitcast.11, s32[]{:T(128)} %bitcast.10, s32[]{:T(128)} %bitcast.9, s32[]{:T(128)} %bitcast.8, s32[]{:T(128)} %bitcast.7, s32[]{:T(128)} %bitcast.6, s32[]{:T(128)} %bitcast.5), kind=kLoop, calls=%fused_computation.99 | loop fusion | flops 4224 | bytes 1184 | tf_op jit(solution)/shard_map/jit(_take)/and | solution.py:127
  56.2 2.7 pad_maximum_fusion
  59.0 0.9 bitcast_reduce_fusion
  60.3 1.1 fusion.1
  61.4 1.4 fusion.21
  63.0 0.8 gather_fusion.4
  64.1 20.8 %all_to_all.31 = bf16[8,128,512]{2,1,0:T(8,128)(2,1)S(1)} all-to-all(bf16[8,128,512]{2,1,0:T(8,128)(2,1)S(1)} %broadcast_in_dim.122), channel_id=1, replica_groups=mesh['replica'=8,'tensor'=16] {'replica'}, dimensions={0} | all-to-all | bytes 2097152 | tf_op jit(solution)/shard_map/all_to_all | solution.py:128
  84.9 4.3 %convolution_convert_fusion.1 = bf16[1024,2048]{1,0:T(8,128)(2,1)} fusion(bf16[1024,512]{1,0:T(8,128)(2,1)S(1)} %bitcast.148, bf16[512,2048]{1,0:T(8,128)(2,1)S(1)} %copy-done), kind=kOutput, calls=%fused_computation.13 | convolution fusion | flops 2149580800 | bytes 7340032 | tf_op jit(solution)/shard_map/dot_general | solution.py:135
  89.2 7.2 %all-to-all-start.2 = ((bf16[16,64,2048]{2,1,0:T(8,128)(2,1)}), bf16[16,64,2048]{2,1,0:T(8,128)(2,1)}, u32[]{:S(2)}, u32[]{:S(2)}) async-start(bf16[16,64,2048]{2,1,0:T(8,128)(2,1)} %bitcast.147), calls=%async_computation.2 | async-start | bytes 8388608 | tf_op jit(solution)/shard_map/all_to_all | solution.py:139
  96.4 57.9 %all-to-all-done.2 = bf16[16,64,2048]{2,1,0:T(8,128)(2,1)} async-done(((bf16[16,64,2048]{2,1,0:T(8,128)(2,1)}), bf16[16,64,2048]{2,1,0:T(8,128)(2,1)}, u32[]{:S(2)}, u32[]{:S(2)}) %all-to-all-start.2) | async-done | bytes 4194336 | tf_op jit(solution)/shard_map/all_to_all | solution.py:139
  154.3 3.0 convert_reduce_fusion.1
  157.3 1.1 multiply_reduce_fusion
  159.0 3.5 %all-to-all-start.3 = ((f32[8,1,64]{2,1,0:T(1,128)}), f32[8,1,64]{2,1,0:T(1,128)S(1)}, u32[]{:S(2)}, u32[]{:S(2)}) async-start(f32[8,1,64]{2,1,0:T(1,128)} %broadcast_in_dim.123), calls=%async_computation.3 | async-start | bytes 8192 | tf_op jit(solution)/shard_map/all_to_all | solution.py:152
  162.6 7.3 %all-to-all-done.3 = f32[8,1,64]{2,1,0:T(1,128)S(1)} async-done(((f32[8,1,64]{2,1,0:T(1,128)}), f32[8,1,64]{2,1,0:T(1,128)S(1)}, u32[]{:S(2)}, u32[]{:S(2)}) %all-to-all-start.3) | async-done | bytes 2080 | tf_op jit(solution)/shard_map/all_to_all | solution.py:152
  169.9 1.1 multiply_convert_fusion
  171.0 2.5 stack.2
  173.5 5.7 %all-to-all-start.4 = ((bf16[16,64,2048]{2,1,0:T(8,128)(2,1)}), bf16[16,64,2048]{2,1,0:T(8,128)(2,1)}, u32[]{:S(2)}, u32[]{:S(2)}) async-start(bf16[16,64,2048]{2,1,0:T(8,128)(2,1)} %stack.2), calls=%async_computation.4 | async-start | bytes 8388608 | tf_op jit(solution)/shard_map/all_to_all | solution.py:165
  179.2 14.2 %copy.57 = bf16[256,8,2,1664]{3,1,2,0:T(8,128)(2,1)} copy(bf16[256,8,2,1664]{3,2,1,0:T(2,128)(2,1)} %bitcast.140) | data formatting | bytes 27262976
  193.5 44.9 %all-to-all-done.4 = bf16[16,64,2048]{2,1,0:T(8,128)(2,1)} async-done(((bf16[16,64,2048]{2,1,0:T(8,128)(2,1)}), bf16[16,64,2048]{2,1,0:T(8,128)(2,1)}, u32[]{:S(2)}, u32[]{:S(2)}) %all-to-all-start.4) | async-done | bytes 4194336 | tf_op jit(solution)/shard_map/all_to_all | solution.py:165
  238.4 19.7 %convolution_convert_fusion = bf16[1024,3328]{1,0:T(8,128)(2,1)S(1)} fusion(bf16[1024,2048]{1,0:T(8,128)(2,1)} %bitcast.42, bf16[2048,3328]{1,0:T(8,128)(2,1)} %bitcast.141), kind=kOutput, calls=%fused_computation.7 | convolution fusion | flops 13962051584 | bytes 24641536 | tf_op jit(solution)/shard_map/dot_general | solution.py:169
  258.1 82.5 %all_to_all.32 = bf16[8,128,3328]{2,1,0:T(8,128)(2,1)S(1)} all-to-all(bf16[8,128,3328]{2,1,0:T(8,128)(2,1)S(1)} %bitcast.143), channel_id=1, replica_groups=mesh['replica'=8,'tensor'=16] {'replica'}, dimensions={0} | all-to-all | bytes 13631488 | tf_op jit(solution)/shard_map/all_to_all | solution.py:170
  340.7 0.9 convert_reduce_fusion
  341.6 1.0 fusion.24
  (55 shorter events, 7.9 us)
Async XLA Ops:
  0.0 84.9 %copy-start = (bf16[512,2048]{1,0:T(8,128)(2,1)S(1)}, bf16[512,2048]{1,0:T(8,128)(2,1)}, u32[]{:S(2)}) copy-start(bf16[512,2048]{1,0:T(8,128)(2,1)} %param.18) | copy-start | bytes 6291460
  7.9 39.9 %copy-start.4 = (s32[64]{0:T(128)S(1)}, s32[64]{0:T(128)}, u32[]{:S(2)}) copy-start(s32[64]{0:T(128)} %param.16) | copy-start | bytes 772
  7.9 40.0 %copy-start.2 = (bf16[128,512]{1,0:T(8,128)(2,1)S(1)}, bf16[128,512]{1,0:T(8,128)(2,1)}, u32[]{:S(2)}) copy-start(bf16[128,512]{1,0:T(8,128)(2,1)} %param.11) | copy-start | bytes 393220
  9.5 37.9 %all-to-all-start = ((bf16[128,1,32,256]{3,2,1,0:T(8,128)(2,1)}), bf16[128,1,32,256]{3,2,1,0:T(8,128)(2,1)}, u32[]{:S(2)}, u32[]{:S(2)}) async-start(bf16[128,1,32,256]{3,2,1,0:T(8,128)(2,1)} %bitcast.142), calls=%async_computation | async-start | bytes 4194304 | tf_op jit(solution)/shard_map/all_to_all | solution.py:51
  47.3 8.9 %collective-permute-start = (bf16[128,1,32,256]{3,2,1,0:T(8,128)(2,1)}, bf16[128,1,32,256]{3,2,1,0:T(8,128)(2,1)}, u32[]{:S(2)}, u32[]{:S(2)}) collective-permute-start(bf16[128,1,32,256]{3,2,1,0:T(8,128)(2,1)} %all-to-all-done), channel_id=1, source_target_pairs={{0,1},{1,0},{2,3},{3,2},{4,5},{5,4},{6,7},{7,6},{8,9},{9,8},{10,11... | collective-permute-start | bytes 6291464 | tf_op jit(solution)/shard_map/ppermute | solution.py:54
  89.2 65.1 %all-to-all-start.2 = ((bf16[16,64,2048]{2,1,0:T(8,128)(2,1)}), bf16[16,64,2048]{2,1,0:T(8,128)(2,1)}, u32[]{:S(2)}, u32[]{:S(2)}) async-start(bf16[16,64,2048]{2,1,0:T(8,128)(2,1)} %bitcast.147), calls=%async_computation.2 | async-start | bytes 8388608 | tf_op jit(solution)/shard_map/all_to_all | solution.py:139
  96.4 66.1 %copy-start.3 = (bf16[2048]{0:T(1024)(128)(2,1)S(1)}, bf16[2048]{0:T(1024)(128)(2,1)}, u32[]{:S(2)}) copy-start(bf16[2048]{0:T(1024)(128)(2,1)} %param.20) | copy-start | bytes 12292
  159.0 10.9 %all-to-all-start.3 = ((f32[8,1,64]{2,1,0:T(1,128)}), f32[8,1,64]{2,1,0:T(1,128)S(1)}, u32[]{:S(2)}, u32[]{:S(2)}) async-start(f32[8,1,64]{2,1,0:T(1,128)} %broadcast_in_dim.123), calls=%async_computation.3 | async-start | bytes 8192 | tf_op jit(solution)/shard_map/all_to_all | solution.py:152
  173.5 64.9 %all-to-all-start.4 = ((bf16[16,64,2048]{2,1,0:T(8,128)(2,1)}), bf16[16,64,2048]{2,1,0:T(8,128)(2,1)}, u32[]{:S(2)}, u32[]{:S(2)}) async-start(bf16[16,64,2048]{2,1,0:T(8,128)(2,1)} %stack.2), calls=%async_computation.4 | async-start | bytes 8388608 | tf_op jit(solution)/shard_map/all_to_all | solution.py:165
  258.1 84.5 %copy-start.1 = (bf16[512,2048]{1,0:T(8,128)(2,1)S(1)}, bf16[512,2048]{1,0:T(8,128)(2,1)}, u32[]{:S(2)}) copy-start(bf16[512,2048]{1,0:T(8,128)(2,1)} %param.18) | copy-start | bytes 6291460
